TPU v7x, 32 devices: a whole 2x2x4 slice. The times are simulated.
32 devices in a mesh: pb: 8 (over z, y), ka: 4 (over x, core).
Axes of the slice: x: 2, y: 2, z: 4, core: 2. Of those that a mesh axis runs over, the one named last changes fastest.
Arguments:
- query_rows: bfloat16 [4096, 512], P(('pb', 'ka')), may hold values from -8 to 8
- key_rows: bfloat16 [4096, 128], P(('pb', 'ka')), may hold values from -3 to 3
- value_rows: bfloat16 [4096, 128], P(('pb', 'ka')), may hold values from -6 to 6
- outputs: bfloat16 [4096, 512], P(('pb', 'ka')), may hold values from -3 to 3
- out_grads: bfloat16 [4096, 512], P(('pb', 'ka')), may hold values from -6 to 6
- log_totals: float32 [4, 4096], P(None, ('pb', 'ka'))
- selected: int32 [32, 2], P(('pb', 'ka')), may hold values from 0 to 31, as said below
- counts: int32 [32], P(('pb', 'ka')), may hold values from 1 to 2, as said below
Outputs:
- query_grad: float32 [4096, 512], P(('pb', 'ka'))
- key_grad: float32 [4096, 128], P(('pb', 'ka'))
- value_grad: float32 [4096, 128], P(('pb', 'ka'))
Inputs may be any that keep to these rules, and one draw needn't show every extreme that they name: `selected`: slot 0 of row q is q itself; the first counts[q] entries of row q are distinct blocks no later than q; entries from slot counts[q] on are padding and are ignored. counts[q] is at most q + 1; the last query block's count is 2.
All inputs are finite; a program needn't handle non-finite values.
Results may differ from a plain program's by a relative error of at most 0.0029.
Values may be sent and summed in bfloat16 or wider, within the bound.
A program may use at most 64 MiB of HBM per device.

v0:
```python
import jax
import jax.numpy as jnp
from jax import lax
from jax.sharding import PartitionSpec as P

VERY_LOW = -1e30


def passed_along(value, axis, steps):
    count = lax.axis_size(axis)
    pairs = [(source, (source + steps) % count) for source in range(count)]
    return lax.ppermute(value, axis, pairs)


def head_sums(grad_rows, out_rows, head_width):
    row_total = grad_rows.shape[0]
    part_heads = grad_rows.shape[1] // head_width
    product = grad_rows.astype(jnp.float32) * out_rows.astype(jnp.float32)
    return jnp.sum(product.reshape(row_total, part_heads, head_width), axis=2).T


def shards(query_rows, key_rows, value_rows, outputs, out_grads, log_totals, selected, counts):
    ka_count = lax.axis_size("ka")
    ka_index = lax.axis_index("ka")
    pb_index = lax.axis_index("pb")
    block_count = selected.shape[0]
    slot_count = selected.shape[1]
    head_width = key_rows.shape[1]
    block_rows = query_rows.shape[0] // block_count
    score_scale = head_width ** (-0.5)
    key_pairs = jnp.concatenate([key_rows, value_rows], 1)
    column_keys = lax.all_gather(key_pairs, "pb", axis=0, tiled=True)
    peer_slots, peer_counts = (
        lax.all_gather(selected, "ka", axis=0, tiled=True),
        lax.all_gather(counts, "ka", axis=0, tiled=True),
    )
    key_grads = jnp.zeros((column_keys.shape[0], 2 * head_width), jnp.float32)
    row_offsets = jnp.arange(block_rows, dtype=jnp.int32)
    flat_owner = jnp.repeat(jnp.arange(block_count, dtype=jnp.int32), slot_count)
    flat_slot = jnp.tile(jnp.arange(slot_count, dtype=jnp.int32), block_count)
    flat_places = jnp.arange(block_count * slot_count, dtype=jnp.int32)

    def visit_block(row_stack, query_grad, stat_stack, anchor, key_grads):
        held_query = row_stack[0]
        held_grad = row_stack[1]
        total_rows = stat_stack[0]
        delta_rows = head_sums(row_stack[1], row_stack[2], head_width)
        part_heads = total_rows.shape[0]
        held_slots = lax.dynamic_slice_in_dim(
            peer_slots, anchor * block_count, block_count, 0
        ).reshape(-1)
        held_counts = jnp.repeat(
            lax.dynamic_slice_in_dim(peer_counts, anchor * block_count, block_count, 0), slot_count
        )
        first_block = (pb_index * ka_count + anchor) * block_count
        wanted = (flat_slot < held_counts) & (held_slots // block_count % ka_count == ka_index)
        position = jnp.cumsum(wanted.astype(jnp.int32)) - 1
        placed = wanted[:, None] & (position[:, None] == flat_places[None, :])
        packed_ids = jnp.sum(jnp.where(placed, held_slots[:, None], 0), axis=0)
        packed_owner = jnp.sum(jnp.where(placed, flat_owner[:, None], 0), axis=0)
        live_tiles = jnp.sum(wanted.astype(jnp.int32))

        def one_tile(tile_index, loop_state):
            query_grad, key_grads = loop_state
            key_block = packed_ids[tile_index]
            owner_block = packed_owner[tile_index]
            key_start = (
                key_block // (block_count * ka_count) * block_count + key_block % block_count
            ) * block_rows
            pair_tile = lax.dynamic_slice_in_dim(column_keys, key_start, block_rows, 0)
            key_tile = pair_tile[:, :head_width]
            value_tile = pair_tile[:, head_width:]
            query_tile = held_query.reshape(block_rows, part_heads, head_width)
            grad_tile = held_grad.reshape(block_rows, part_heads, head_width)
            scores = (
                jnp.einsum("rhd,cd->hrc", query_tile, key_tile, preferred_element_type=jnp.float32)
                * score_scale
            )
            query_pos = (first_block + owner_block) * block_rows + row_offsets
            key_pos = key_block * block_rows + row_offsets
            allowed = key_pos[None, :] <= query_pos[:, None]
            probs_full = jnp.exp(
                jnp.where(allowed[None], scores - total_rows[:, :, None], VERY_LOW)
            )
            prob_grads = jnp.einsum(
                "rhd,cd->hrc", grad_tile, value_tile, preferred_element_type=jnp.float32
            )
            score_grads = probs_full * (prob_grads - delta_rows[:, :, None])
            rounded_probs = probs_full.astype(jnp.bfloat16)
            rounded_grads = score_grads.astype(jnp.bfloat16)
            value_part = jnp.einsum(
                "hrc,rhd->cd", rounded_probs, grad_tile, preferred_element_type=jnp.float32
            )
            key_part = (
                jnp.einsum(
                    "hrc,rhd->cd", rounded_grads, query_tile, preferred_element_type=jnp.float32
                )
                * score_scale
            )
            query_part = (
                jnp.einsum(
                    "hrc,cd->rhd", rounded_grads, key_tile, preferred_element_type=jnp.float32
                )
                * score_scale
            )
            old_query = query_grad
            query_grad = old_query + query_part.reshape(block_rows, -1)
            old_keys = lax.dynamic_slice_in_dim(key_grads, key_start, block_rows, 0)
            key_grads = lax.dynamic_update_slice_in_dim(
                key_grads, old_keys + jnp.concatenate([key_part, value_part], 1), key_start, 0
            )
            return (query_grad, key_grads)

        return lax.fori_loop(0, live_tiles, one_tile, (query_grad, key_grads))

    query_part = query_rows
    grad_zero = jnp.zeros(query_part.shape, jnp.float32)
    row_stack = jnp.stack([query_part, out_grads, outputs])
    query_grad = grad_zero
    stat_stack = log_totals[None]

    def forward_hop(hop_index, loop_state):
        row_stack, query_grad, stat_stack, key_grads = loop_state
        anchor = (ka_index - hop_index) % ka_count
        query_grad, key_grads = visit_block(row_stack, query_grad, stat_stack, anchor, key_grads)
        row_stack = passed_along(row_stack, "ka", 1)
        query_grad, stat_stack = passed_along((query_grad, stat_stack), "ka", 1)
        return (row_stack, query_grad, stat_stack, key_grads)

    row_stack, query_grad, stat_stack, key_grads = lax.fori_loop(
        0, ka_count - 1, forward_hop, (row_stack, query_grad, stat_stack, key_grads)
    )
    query_grad, key_grads = visit_block(
        row_stack, query_grad, stat_stack, (ka_index + 1) % ka_count, key_grads
    )
    query_grad = passed_along(query_grad, "ka", 1)
    owned_grads = lax.psum_scatter(key_grads, "pb", scatter_dimension=0, tiled=True)
    return (query_grad, owned_grads[:, :head_width], owned_grads[:, head_width:])


def solution(mesh):
    return jax.shard_map(
        shards,
        mesh=mesh,
        in_specs=(
            P(("pb", "ka"), None),
            P(("pb", "ka"), None),
            P(("pb", "ka"), None),
            P(("pb", "ka"), None),
            P(("pb", "ka"), None),
            P(None, ("pb", "ka")),
            P(("pb", "ka"), None),
            P(("pb", "ka")),
        ),
        out_specs=(P(("pb", "ka"), None), P(("pb", "ka"), None), P(("pb", "ka"), None)),
        check_vma=False,
    )
```

profile of v0, /device:TPU:0, one launch (start us, length us, event | category | flops | bytes accessed | tf_op | source)
XLA Modules:
  0.0 183.4 jit_solution(7212830723820672716)
XLA Ops:
  9.2 0.8 dynamic-update-slice
  10.0 6.4 %all-reduce = s32[4]{0:T(128)S(1)} all-reduce(s32[4]{0:T(128)S(1)} %dynamic-update-slice), channel_id=1, replica_groups=mesh['pb'=8,'ka'=4] {'ka'}, use_global_device_ids=true, to_apply=%add | all-reduce | flops 4 | bytes 32
  17.0 5.0 %all-gather = s32[4,1,2]{2,1,0:T(1,128)S(1)} all-gather(s32[1,1,2]{2,1,0:T(1,128)S(1)} %bitcast.222), channel_id=1, replica_groups=mesh['pb'=8,'ka'=4] {'ka'}, dimensions={0}, use_global_device_ids=true | all-gather | bytes 40 | tf_op jit(solution)/shard_map/all_gather | solution.py:34
  22.7 1.3 convert_reduce_fusion.1
  24.5 1.1 copy.63
  25.7 0.8 copy-done.2
  27.3 31.9 %all_gather.11 = bf16[1024,256]{1,0:T(8,128)(2,1)S(1)} all-gather(bf16[128,256]{1,0:T(8,128)(2,1)S(1)} %pad_maximum_fusion.1), channel_id=1, replica_groups=mesh['pb'=8,'ka'=4] {'pb'}, dimensions={0}, use_global_device_ids=true | all-gather | bytes 589824 | tf_op jit(solution)/shard_map/all_gather | solution.py:32
  60.0 40.6 %while.86 = (s32[]{:T(128)}, bf16[3,128,512]{1,2,0:T(8,128)(2,1)S(1)}, f32[128,512]{0,1:T(8,128)S(1)}, f32[1,4,128]{2,1,0:T(4,128)S(1)}, f32[1024,256]{0,1:T(8,1...) while((s32[]{:T(128)}, ...), condition=%wide.region_7.8_spmd.clone.clone, body=%wide.region_0.7_spmd.clone.clone.sunk | while | flops 84836216 | bytes 8673559 | solution.py:130
  60.7 1.3 convert_reduce_fusion.3
  63.1 6.2 %while.88 = (s32[]{:T(128)}, f32[128,512]{0,1:T(8,128)S(1)}, f32[1024,256]{0,1:T(8,128)S(1)}, s32[]{:T(128)}, s32[2]{0:T(128)S(1)}, /*index=5*/bf16[1024,256]{1,...) while((s32[]{:T(128)}, f32[128,512]{0,1:T(8,128)S(1)}, ...), condition=%wide.region_6.6_spmd.clone, body=%wide.region_5.5_spmd.clone.sunk | while | flops 84574488 | bytes 3415011 | solution.py:114
  69.3 1.0 collective-permute-start.1
  70.3 4.8 %collective-permute-done.1 = f32[128,512]{0,1:T(8,128)S(1)} collective-permute-done((f32[128,512]{0,1:T(8,128)S(1)}, f32[128,512]{0,1:T(8,128)S(1)}, u32[]{:S(2)}, u32[]{:S(2)}) %collective-permute-start.1) | collective-permute-done | bytes 262176 | tf_op jit(solution)/shard_map/while/body/eval_jaxpr/ppermute | solution.py:12
  76.0 1.3 convert_reduce_fusion.3
  78.9 1.0 collective-permute-start.1
  80.0 5.3 %collective-permute-done.1 = f32[128,512]{0,1:T(8,128)S(1)} collective-permute-done((f32[128,512]{0,1:T(8,128)S(1)}, f32[128,512]{0,1:T(8,128)S(1)}, u32[]{:S(2)}, u32[]{:S(2)}) %collective-permute-start.1) | collective-permute-done | bytes 262176 | tf_op jit(solution)/shard_map/while/body/eval_jaxpr/ppermute | solution.py:12
  86.1 1.3 convert_reduce_fusion.3
  88.4 6.2 %while.88 = (s32[]{:T(128)}, f32[128,512]{0,1:T(8,128)S(1)}, f32[1024,256]{0,1:T(8,128)S(1)}, s32[]{:T(128)}, s32[2]{0:T(128)S(1)}, /*index=5*/bf16[1024,256]{1,...) while((s32[]{:T(128)}, f32[128,512]{0,1:T(8,128)S(1)}, ...), condition=%wide.region_6.6_spmd.clone, body=%wide.region_5.5_spmd.clone.sunk | while | flops 84574488 | bytes 3415011 | solution.py:114
  94.7 1.0 collective-permute-start.1
  95.7 4.8 %collective-permute-done.1 = f32[128,512]{0,1:T(8,128)S(1)} collective-permute-done((f32[128,512]{0,1:T(8,128)S(1)}, f32[128,512]{0,1:T(8,128)S(1)}, u32[]{:S(2)}, u32[]{:S(2)}) %collective-permute-start.1) | collective-permute-done | bytes 262176 | tf_op jit(solution)/shard_map/while/body/eval_jaxpr/ppermute | solution.py:12
  100.9 6.4 %while.87 = (s32[]{:T(128)}, f32[128,512]{0,1:T(8,128)S(1)}, f32[1024,256]{0,1:T(8,128)S(1)}, s32[]{:T(128)}, s32[2]{0:T(128)S(1)}, /*index=5*/bf16[1024,256]{1,...) while((s32[]{:T(128)}, f32[128,512]{0,1:T(8,128)S(1)}, ...), condition=%wide.region_13.14_spmd.clone.clone, body=%wide.region_12.13_spmd.clone.clone.sunk | while | flops 84574488 | bytes 3414491 | solution.py:114
  107.4 1.3 copy.67
  108.9 5.8 %collective-permute-done.3 = f32[128,512]{1,0:T(8,128)S(1)} collective-permute-done((f32[128,512]{1,0:T(8,128)S(1)}, f32[128,512]{1,0:T(8,128)S(1)}, u32[]{:S(2)}, u32[]{:S(2)}) %collective-permute-start.3) | collective-permute-done | bytes 262176 | tf_op jit(solution)/shard_map/ppermute | solution.py:12
  114.7 59.6 %reduce-scatter.2.cloned.1.call-done = f32[128,256]{1,0:T(8,128)} async-done(((f32[1024,256]{1,0:T(8,128)}), f32[128,256]{1,0:T(8,128)}) %reduce-scatter.2.cloned.1.call-update) | async-done | bytes 131088 | tf_op jit(solution)/shard_map/reduce_scatter | solution.py:137
  174.3 1.5 fusion.43
  (113 shorter events, 17.3 us)
Async XLA Ops:
  7.2 167.1 %reduce-scatter.2.cloned.1.call-start = ((), (), s32[]{:S(2)}) async-start(), calls=%async_computation.1 | async-start | bytes 1179648 | tf_op jit(solution)/shard_map/reduce_scatter | solution.py:137
  7.9 0.7 copy-start.6
  16.4 0.7 copy-start.5
  24.5 1.1 copy-start.1
  25.6 0.9 copy-start.2
  26.5 0.8 copy-start.3
  26.5 0.8 copy-start.4
  59.3 0.7 copy-start
  60.0 15.2 %collective-permute-start = (bf16[3,128,512]{1,2,0:T(8,128)(2,1)S(1)}, bf16[3,128,512]{1,2,0:T(8,128)(2,1)S(1)}, u32[]{:S(2)}, u32[]{:S(2)}) collective-permute-start(bf16[3,128,512]{1,2,0:T(8,128)(2,1)S(1)} %copy.101), channel_id=1, source_target_pairs={{0,1},{1,2},{2,3},{3,0},{4,5},{5,6},{6,7},{7,4},{8,9},{9,10},{10,1... | collective-permute-start | bytes 1179656 | tf_op jit(solution)/shard_map/while/body/eval_jaxpr/ppermute | solution.py:12
  69.3 5.8 %collective-permute-start.1 = (f32[128,512]{0,1:T(8,128)S(1)}, f32[128,512]{0,1:T(8,128)S(1)}, u32[]{:S(2)}, u32[]{:S(2)}) collective-permute-start(f32[128,512]{0,1:T(8,128)S(1)} %get-tuple-element.1444), channel_id=1, source_target_pairs={{0,1},{1,2},{2,3},{3,0},{4,5},{5,6},{6,7},{7,4},{8,9},{9,10},{10,1... | collective-permute-start | bytes 786440 | tf_op jit(solution)/shard_map/while/body/eval_jaxpr/ppermute | solution.py:12
  70.3 4.9 %collective-permute-start.2 = (f32[1,4,128]{2,1,0:T(4,128)S(1)}, f32[1,4,128]{2,1,0:T(4,128)S(1)}, u32[]{:S(2)}, u32[]{:S(2)}) collective-permute-start(f32[1,4,128]{2,1,0:T(4,128)S(1)} %get-tuple-element.1678), channel_id=1, source_target_pairs={{0,1},{1,2},{2,3},{3,0},{4,5},{5,6},{6,7},{7,4},{8,9},{9,10},{10,1... | collective-permute-start | bytes 6152 | tf_op jit(solution)/shard_map/while/body/eval_jaxpr/ppermute | solution.py:12
  75.2 10.1 %collective-permute-start = (bf16[3,128,512]{1,2,0:T(8,128)(2,1)S(1)}, bf16[3,128,512]{1,2,0:T(8,128)(2,1)S(1)}, u32[]{:S(2)}, u32[]{:S(2)}) collective-permute-start(bf16[3,128,512]{1,2,0:T(8,128)(2,1)S(1)} %copy.101), channel_id=1, source_target_pairs={{0,1},{1,2},{2,3},{3,0},{4,5},{5,6},{6,7},{7,4},{8,9},{9,10},{10,1... | collective-permute-start | bytes 1179656 | tf_op jit(solution)/shard_map/while/body/eval_jaxpr/ppermute | solution.py:12
  78.9 6.3 %collective-permute-start.1 = (f32[128,512]{0,1:T(8,128)S(1)}, f32[128,512]{0,1:T(8,128)S(1)}, u32[]{:S(2)}, u32[]{:S(2)}) collective-permute-start(f32[128,512]{0,1:T(8,128)S(1)} %get-tuple-element.1444), channel_id=1, source_target_pairs={{0,1},{1,2},{2,3},{3,0},{4,5},{5,6},{6,7},{7,4},{8,9},{9,10},{10,1... | collective-permute-start | bytes 786440 | tf_op jit(solution)/shard_map/while/body/eval_jaxpr/ppermute | solution.py:12
  79.9 5.4 %collective-permute-start.2 = (f32[1,4,128]{2,1,0:T(4,128)S(1)}, f32[1,4,128]{2,1,0:T(4,128)S(1)}, u32[]{:S(2)}, u32[]{:S(2)}) collective-permute-start(f32[1,4,128]{2,1,0:T(4,128)S(1)} %get-tuple-element.1678), channel_id=1, source_target_pairs={{0,1},{1,2},{2,3},{3,0},{4,5},{5,6},{6,7},{7,4},{8,9},{9,10},{10,1... | collective-permute-start | bytes 6152 | tf_op jit(solution)/shard_map/while/body/eval_jaxpr/ppermute | solution.py:12
  85.4 15.2 %collective-permute-start = (bf16[3,128,512]{1,2,0:T(8,128)(2,1)S(1)}, bf16[3,128,512]{1,2,0:T(8,128)(2,1)S(1)}, u32[]{:S(2)}, u32[]{:S(2)}) collective-permute-start(bf16[3,128,512]{1,2,0:T(8,128)(2,1)S(1)} %copy.101), channel_id=1, source_target_pairs={{0,1},{1,2},{2,3},{3,0},{4,5},{5,6},{6,7},{7,4},{8,9},{9,10},{10,1... | collective-permute-start | bytes 1179656 | tf_op jit(solution)/shard_map/while/body/eval_jaxpr/ppermute | solution.py:12
  94.7 5.8 %collective-permute-start.1 = (f32[128,512]{0,1:T(8,128)S(1)}, f32[128,512]{0,1:T(8,128)S(1)}, u32[]{:S(2)}, u32[]{:S(2)}) collective-permute-start(f32[128,512]{0,1:T(8,128)S(1)} %get-tuple-element.1444), channel_id=1, source_target_pairs={{0,1},{1,2},{2,3},{3,0},{4,5},{5,6},{6,7},{7,4},{8,9},{9,10},{10,1... | collective-permute-start | bytes 786440 | tf_op jit(solution)/shard_map/while/body/eval_jaxpr/ppermute | solution.py:12
  95.6 4.9 %collective-permute-start.2 = (f32[1,4,128]{2,1,0:T(4,128)S(1)}, f32[1,4,128]{2,1,0:T(4,128)S(1)}, u32[]{:S(2)}, u32[]{:S(2)}) collective-permute-start(f32[1,4,128]{2,1,0:T(4,128)S(1)} %get-tuple-element.1678), channel_id=1, source_target_pairs={{0,1},{1,2},{2,3},{3,0},{4,5},{5,6},{6,7},{7,4},{8,9},{9,10},{10,1... | collective-permute-start | bytes 6152 | tf_op jit(solution)/shard_map/while/body/eval_jaxpr/ppermute | solution.py:12
  108.9 5.8 %collective-permute-start.3 = (f32[128,512]{1,0:T(8,128)S(1)}, f32[128,512]{1,0:T(8,128)S(1)}, u32[]{:S(2)}, u32[]{:S(2)}) collective-permute-start(f32[128,512]{1,0:T(8,128)S(1)} %copy.66), channel_id=1, source_target_pairs={{0,1},{1,2},{2,3},{3,0},{4,5},{5,6},{6,7},{7,4},{8,9},{9,10},{10,1... | collective-permute-start | bytes 786440 | tf_op jit(solution)/shard_map/ppermute | solution.py:12
Sparse Core Ops, SparseCore 0:
  108.9 65.3 reduce-scatter.1
where the time goes:
time: 184 us; the launch traced here: 183 us
  waiting for transfers between devices  80.3 us (44%)
  blocking collectives  43.3 us (24%)
  between operations  14.8 us (8%)
  loops' own time  14.6 us (8%)
  local copies, waits for them, and re-layouts  14.4 us (8%)
  other arithmetic  9.58 us (5%)
  starting transfers between devices  3.4 us (2%)
  matrix products  2.9 us (2%)
    reduce_scatter x1, waiting for transfers between devices, shards(): lax.psum_scatter(key_grads, 'pb', scatter_dimension=0, tiled=True)  59.6 us
    all_gather x1, blocking collectives, shards(): column_keys = lax.all_gather(key_pairs, 'pb', axis=0, tiled=True)  31.9 us
    ppermute x10, waiting for transfers between devices, passed_along(): return lax.ppermute(value, axis, pairs)  20.7 us
    another operation x4, loops' own time, visit_block(): return lax.fori_loop(0, live_tiles, one_tile, (query_grad, key_grads))  14.3 us
    unnamed x21, local copies, waits for them, and re-layouts  6.74 us
    unnamed x1, blocking collectives  6.38 us
    reduce_sum x4, other arithmetic, visit_block(): live_tiles = jnp.sum(wanted.astype(jnp.int32))  5.18 us
    all_gather x1, blocking collectives, shards(): lax.all_gather(selected, 'ka', axis=0, tiled=True)  5.05 us
  transfers between devices with their start and end apart: 11, of which 5 were waited for; matrix products, arithmetic and copies ran while one was open for 7% of the time, Pallas kernels for 0%

commit v1 on v0

--- a/solution.py
+++ b/solution.py
@@ -29,7 +29,10 @@
     block_rows = query_rows.shape[0] // block_count
     score_scale = head_width ** (-0.5)
     key_pairs = jnp.concatenate([key_rows, value_rows], 1)
-    column_keys = lax.all_gather(key_pairs, "pb", axis=0, tiled=True)
+    devices = lax.axis_size("pb")
+    blocks = jnp.stack([key_pairs for _ in range(devices)])
+    blocks = lax.all_to_all(blocks, "pb", split_axis=0, concat_axis=0)
+    column_keys = jnp.concatenate(blocks, axis=0)
     peer_slots, peer_counts = (
         lax.all_gather(selected, "ka", axis=0, tiled=True),
         lax.all_gather(counts, "ka", axis=0, tiled=True),

time: 184 us -> 162 us (0.88)
  blocking collectives: 43.3 us -> 9.95 us
  starting transfers between devices: 3.4 us -> 10.8 us
  waiting for transfers between devices: 80.3 us -> 83.2 us
    all_gather x1 -> x0, blocking collectives: 31.9 us -> none  [shards(): column_keys = lax.all_gather(key_pairs, 'pb', axis=0, tiled=True)]
    all_to_all x0 -> x1, starting transfers between devices: none -> 7.44 us  [shards(): blocks = lax.all_to_all(blocks, 'pb', split_axis=0, concat_axis=0)]
    reduce_scatter x1, waiting for transfers between devices: 59.6 us -> 62.3 us  [shards(): lax.psum_scatter(key_grads, 'pb', scatter_dimension=0, tiled=True)]
    unnamed x21 -> x19, local copies, waits for them, and re-layouts: 6.74 us -> 5.82 us
  transfers between devices with their start and end apart: 11 -> 12, of which waited for: 5 -> 5; matrix products, arithmetic and copies ran while one was open for 7% -> 10% of each run, Pallas kernels for 0% -> 0%
where the time goes in v1:
time: 162 us; the launch traced here: 161 us
  waiting for transfers between devices  83.2 us (51%)
  loops' own time  14.8 us (9%)
  between operations  14.8 us (9%)
  local copies, waits for them, and re-layouts  14.2 us (9%)
  starting transfers between devices  10.8 us (7%)
  other arithmetic  10.1 us (6%)
  blocking collectives  9.95 us (6%)
  matrix products  2.91 us (2%)
    reduce_scatter x1, waiting for transfers between devices, shards(): lax.psum_scatter(key_grads, 'pb', scatter_dimension=0, tiled=True)  62.3 us
    ppermute x10, waiting for transfers between devices, passed_along(): return lax.ppermute(value, axis, pairs)  20.8 us
    another operation x4, loops' own time, visit_block(): return lax.fori_loop(0, live_tiles, one_tile, (query_grad, key_grads))  14.5 us
    all_to_all x1, starting transfers between devices, shards(): blocks = lax.all_to_all(blocks, 'pb', split_axis=0, concat_axis=0)  7.44 us
    unnamed x19, local copies, waits for them, and re-layouts  5.82 us
    reduce_sum x4, other arithmetic, visit_block(): live_tiles = jnp.sum(wanted.astype(jnp.int32))  5.08 us
    all_gather x1, blocking collectives, shards(): lax.all_gather(selected, 'ka', axis=0, tiled=True)  5.05 us
    unnamed x1, blocking collectives  4.9 us
  transfers between devices with their start and end apart: 12, of which 5 were waited for; matrix products, arithmetic and copies ran while one was open for 10% of the time, Pallas kernels for 0%

profile of v1, /device:TPU:0, one launch (start us, length us, event | category | flops | bytes accessed | tf_op | source)
XLA Modules:
  0.0 160.8 jit_solution(6251212711825602742)
XLA Ops:
  7.2 0.8 pad_maximum_fusion.1
  7.9 0.8 stack.27
  8.8 7.4 %all-to-all-start = ((bf16[8,128,256]{2,1,0:T(8,128)(2,1)}), bf16[8,128,256]{2,1,0:T(8,128)(2,1)S(1)}, u32[]{:S(2)}, u32[]{:S(2)}) async-start(bf16[8,128,256]{2,1,0:T(8,128)(2,1)} %stack.27), calls=%async_computation | async-start | bytes 1048576 | tf_op jit(solution)/shard_map/all_to_all | solution.py:34
  19.6 5.0 %all-gather = s32[4,1,2]{2,1,0:T(1,128)S(1)} all-gather(s32[1,1,2]{2,1,0:T(1,128)S(1)} %bitcast.224), channel_id=1, replica_groups=mesh['pb'=8,'ka'=4] {'ka'}, dimensions={0}, use_global_device_ids=true | all-gather | bytes 40 | tf_op jit(solution)/shard_map/all_gather | solution.py:37
  24.6 4.9 %all-reduce = s32[4]{0:T(128)S(1)} all-reduce(s32[4]{0:T(128)S(1)} %dynamic-update-slice), channel_id=1, replica_groups=mesh['pb'=8,'ka'=4] {'ka'}, use_global_device_ids=true, to_apply=%add | all-reduce | flops 4 | bytes 32
  29.6 0.8 copy-done.2
  32.9 1.2 convert_reduce_fusion.1
  35.0 40.7 %while.86 = (s32[]{:T(128)}, bf16[3,128,512]{1,2,0:T(8,128)(2,1)S(1)}, f32[128,512]{0,1:T(8,128)S(1)}, f32[1,4,128]{2,1,0:T(4,128)S(1)}, f32[1024,256]{0,1:T(8,1...) while((s32[]{:T(128)}, ...), condition=%wide.region_7.8_spmd.clone.clone, body=%wide.region_0.7_spmd.clone.clone.sunk | while | flops 84836216 | bytes 8673559 | solution.py:133
  35.7 1.3 convert_reduce_fusion.3
  37.9 6.4 %while.88 = (s32[]{:T(128)}, f32[128,512]{0,1:T(8,128)S(1)}, f32[1024,256]{0,1:T(8,128)S(1)}, s32[]{:T(128)}, s32[2]{0:T(128)S(1)}, /*index=5*/bf16[1024,256]{1,...) while((s32[]{:T(128)}, f32[128,512]{0,1:T(8,128)S(1)}, ...), condition=%wide.region_6.6_spmd.clone, body=%wide.region_5.5_spmd.clone.sunk | while | flops 84574488 | bytes 3415011 | solution.py:117
  44.4 1.0 collective-permute-start.1
  45.4 4.8 %collective-permute-done.1 = f32[128,512]{0,1:T(8,128)S(1)} collective-permute-done((f32[128,512]{0,1:T(8,128)S(1)}, f32[128,512]{0,1:T(8,128)S(1)}, u32[]{:S(2)}, u32[]{:S(2)}) %collective-permute-start.1) | collective-permute-done | bytes 262176 | tf_op jit(solution)/shard_map/while/body/eval_jaxpr/ppermute | solution.py:12
  51.0 1.3 convert_reduce_fusion.3
  53.9 1.0 collective-permute-start.1
  55.0 5.4 %collective-permute-done.1 = f32[128,512]{0,1:T(8,128)S(1)} collective-permute-done((f32[128,512]{0,1:T(8,128)S(1)}, f32[128,512]{0,1:T(8,128)S(1)}, u32[]{:S(2)}, u32[]{:S(2)}) %collective-permute-start.1) | collective-permute-done | bytes 262176 | tf_op jit(solution)/shard_map/while/body/eval_jaxpr/ppermute | solution.py:12
  61.1 1.3 convert_reduce_fusion.3
  63.4 6.4 %while.88 = (s32[]{:T(128)}, f32[128,512]{0,1:T(8,128)S(1)}, f32[1024,256]{0,1:T(8,128)S(1)}, s32[]{:T(128)}, s32[2]{0:T(128)S(1)}, /*index=5*/bf16[1024,256]{1,...) while((s32[]{:T(128)}, f32[128,512]{0,1:T(8,128)S(1)}, ...), condition=%wide.region_6.6_spmd.clone, body=%wide.region_5.5_spmd.clone.sunk | while | flops 84574488 | bytes 3415011 | solution.py:117
  69.8 1.0 collective-permute-start.1
  70.9 4.8 %collective-permute-done.1 = f32[128,512]{0,1:T(8,128)S(1)} collective-permute-done((f32[128,512]{0,1:T(8,128)S(1)}, f32[128,512]{0,1:T(8,128)S(1)}, u32[]{:S(2)}, u32[]{:S(2)}) %collective-permute-start.1) | collective-permute-done | bytes 262176 | tf_op jit(solution)/shard_map/while/body/eval_jaxpr/ppermute | solution.py:12
  75.8 6.2 %while.87 = (s32[]{:T(128)}, f32[128,512]{0,1:T(8,128)S(1)}, f32[1024,256]{0,1:T(8,128)S(1)}, s32[]{:T(128)}, s32[2]{0:T(128)S(1)}, /*index=5*/bf16[1024,256]{1,...) while((s32[]{:T(128)}, f32[128,512]{0,1:T(8,128)S(1)}, ...), condition=%wide.region_13.14_spmd.clone.clone, body=%wide.region_12.13_spmd.clone.clone.sunk | while | flops 84574488 | bytes 3414491 | solution.py:117
  82.0 1.3 copy.67
  83.6 5.8 %collective-permute-done.3 = f32[128,512]{1,0:T(8,128)S(1)} collective-permute-done((f32[128,512]{1,0:T(8,128)S(1)}, f32[128,512]{1,0:T(8,128)S(1)}, u32[]{:S(2)}, u32[]{:S(2)}) %collective-permute-start.3) | collective-permute-done | bytes 262176 | tf_op jit(solution)/shard_map/ppermute | solution.py:12
  89.4 62.3 %reduce-scatter.2.cloned.1.call-done = f32[128,256]{1,0:T(8,128)} async-done(((f32[1024,256]{1,0:T(8,128)}), f32[128,256]{1,0:T(8,128)}) %reduce-scatter.2.cloned.1.call-update) | async-done | bytes 131088 | tf_op jit(solution)/shard_map/reduce_scatter | solution.py:140
  151.7 1.5 fusion.43
  (113 shorter events, 18.1 us)
Async XLA Ops:
  8.8 20.7 %copy-start.1 = (bf16[128,512]{1,0:T(8,128)(2,1)S(1)}, bf16[128,512]{1,0:T(8,128)(2,1)}, u32[]{:S(2)}) copy-start(bf16[128,512]{1,0:T(8,128)(2,1)} %param.17) | copy-start | bytes 393220
  8.8 25.5 %all-to-all-start = ((bf16[8,128,256]{2,1,0:T(8,128)(2,1)}), bf16[8,128,256]{2,1,0:T(8,128)(2,1)S(1)}, u32[]{:S(2)}, u32[]{:S(2)}) async-start(bf16[8,128,256]{2,1,0:T(8,128)(2,1)} %stack.27), calls=%async_computation | async-start | bytes 1048576 | tf_op jit(solution)/shard_map/all_to_all | solution.py:34
  16.2 135.5 %reduce-scatter.2.cloned.1.call-start = ((), (), s32[]{:S(2)}) async-start(), calls=%async_computation.2 | async-start | bytes 1179648 | tf_op jit(solution)/shard_map/reduce_scatter | solution.py:140
  16.9 0.7 copy-start.5
  18.9 0.7 copy-start.4
  29.5 0.9 copy-start.2
  30.4 0.9 copy-start.3
  34.3 0.7 copy-start
  35.0 15.2 %collective-permute-start = (bf16[3,128,512]{1,2,0:T(8,128)(2,1)S(1)}, bf16[3,128,512]{1,2,0:T(8,128)(2,1)S(1)}, u32[]{:S(2)}, u32[]{:S(2)}) collective-permute-start(bf16[3,128,512]{1,2,0:T(8,128)(2,1)S(1)} %copy.101), channel_id=1, source_target_pairs={{0,1},{1,2},{2,3},{3,0},{4,5},{5,6},{6,7},{7,4},{8,9},{9,10},{10,1... | collective-permute-start | bytes 1179656 | tf_op jit(solution)/shard_map/while/body/eval_jaxpr/ppermute | solution.py:12
  44.4 5.8 %collective-permute-start.1 = (f32[128,512]{0,1:T(8,128)S(1)}, f32[128,512]{0,1:T(8,128)S(1)}, u32[]{:S(2)}, u32[]{:S(2)}) collective-permute-start(f32[128,512]{0,1:T(8,128)S(1)} %get-tuple-element.1444), channel_id=1, source_target_pairs={{0,1},{1,2},{2,3},{3,0},{4,5},{5,6},{6,7},{7,4},{8,9},{9,10},{10,1... | collective-permute-start | bytes 786440 | tf_op jit(solution)/shard_map/while/body/eval_jaxpr/ppermute | solution.py:12
  45.4 4.9 %collective-permute-start.2 = (f32[1,4,128]{2,1,0:T(4,128)S(1)}, f32[1,4,128]{2,1,0:T(4,128)S(1)}, u32[]{:S(2)}, u32[]{:S(2)}) collective-permute-start(f32[1,4,128]{2,1,0:T(4,128)S(1)} %get-tuple-element.1679), channel_id=1, source_target_pairs={{0,1},{1,2},{2,3},{3,0},{4,5},{5,6},{6,7},{7,4},{8,9},{9,10},{10,1... | collective-permute-start | bytes 6152 | tf_op jit(solution)/shard_map/while/body/eval_jaxpr/ppermute | solution.py:12
  50.3 10.1 %collective-permute-start = (bf16[3,128,512]{1,2,0:T(8,128)(2,1)S(1)}, bf16[3,128,512]{1,2,0:T(8,128)(2,1)S(1)}, u32[]{:S(2)}, u32[]{:S(2)}) collective-permute-start(bf16[3,128,512]{1,2,0:T(8,128)(2,1)S(1)} %copy.101), channel_id=1, source_target_pairs={{0,1},{1,2},{2,3},{3,0},{4,5},{5,6},{6,7},{7,4},{8,9},{9,10},{10,1... | collective-permute-start | bytes 1179656 | tf_op jit(solution)/shard_map/while/body/eval_jaxpr/ppermute | solution.py:12
  53.9 6.5 %collective-permute-start.1 = (f32[128,512]{0,1:T(8,128)S(1)}, f32[128,512]{0,1:T(8,128)S(1)}, u32[]{:S(2)}, u32[]{:S(2)}) collective-permute-start(f32[128,512]{0,1:T(8,128)S(1)} %get-tuple-element.1444), channel_id=1, source_target_pairs={{0,1},{1,2},{2,3},{3,0},{4,5},{5,6},{6,7},{7,4},{8,9},{9,10},{10,1... | collective-permute-start | bytes 786440 | tf_op jit(solution)/shard_map/while/body/eval_jaxpr/ppermute | solution.py:12
  54.9 5.5 %collective-permute-start.2 = (f32[1,4,128]{2,1,0:T(4,128)S(1)}, f32[1,4,128]{2,1,0:T(4,128)S(1)}, u32[]{:S(2)}, u32[]{:S(2)}) collective-permute-start(f32[1,4,128]{2,1,0:T(4,128)S(1)} %get-tuple-element.1679), channel_id=1, source_target_pairs={{0,1},{1,2},{2,3},{3,0},{4,5},{5,6},{6,7},{7,4},{8,9},{9,10},{10,1... | collective-permute-start | bytes 6152 | tf_op jit(solution)/shard_map/while/body/eval_jaxpr/ppermute | solution.py:12
  60.5 15.2 %collective-permute-start = (bf16[3,128,512]{1,2,0:T(8,128)(2,1)S(1)}, bf16[3,128,512]{1,2,0:T(8,128)(2,1)S(1)}, u32[]{:S(2)}, u32[]{:S(2)}) collective-permute-start(bf16[3,128,512]{1,2,0:T(8,128)(2,1)S(1)} %copy.101), channel_id=1, source_target_pairs={{0,1},{1,2},{2,3},{3,0},{4,5},{5,6},{6,7},{7,4},{8,9},{9,10},{10,1... | collective-permute-start | bytes 1179656 | tf_op jit(solution)/shard_map/while/body/eval_jaxpr/ppermute | solution.py:12
  69.8 5.8 %collective-permute-start.1 = (f32[128,512]{0,1:T(8,128)S(1)}, f32[128,512]{0,1:T(8,128)S(1)}, u32[]{:S(2)}, u32[]{:S(2)}) collective-permute-start(f32[128,512]{0,1:T(8,128)S(1)} %get-tuple-element.1444), channel_id=1, source_target_pairs={{0,1},{1,2},{2,3},{3,0},{4,5},{5,6},{6,7},{7,4},{8,9},{9,10},{10,1... | collective-permute-start | bytes 786440 | tf_op jit(solution)/shard_map/while/body/eval_jaxpr/ppermute | solution.py:12
  70.8 4.9 %collective-permute-start.2 = (f32[1,4,128]{2,1,0:T(4,128)S(1)}, f32[1,4,128]{2,1,0:T(4,128)S(1)}, u32[]{:S(2)}, u32[]{:S(2)}) collective-permute-start(f32[1,4,128]{2,1,0:T(4,128)S(1)} %get-tuple-element.1679), channel_id=1, source_target_pairs={{0,1},{1,2},{2,3},{3,0},{4,5},{5,6},{6,7},{7,4},{8,9},{9,10},{10,1... | collective-permute-start | bytes 6152 | tf_op jit(solution)/shard_map/while/body/eval_jaxpr/ppermute | solution.py:12
  83.5 5.8 %collective-permute-start.3 = (f32[128,512]{1,0:T(8,128)S(1)}, f32[128,512]{1,0:T(8,128)S(1)}, u32[]{:S(2)}, u32[]{:S(2)}) collective-permute-start(f32[128,512]{1,0:T(8,128)S(1)} %copy.66), channel_id=1, source_target_pairs={{0,1},{1,2},{2,3},{3,0},{4,5},{5,6},{6,7},{7,4},{8,9},{9,10},{10,1... | collective-permute-start | bytes 786440 | tf_op jit(solution)/shard_map/ppermute | solution.py:12
Sparse Core Ops, SparseCore 0:
  83.5 68.1 reduce-scatter.1
